TPU v7x, 128 devices: a whole 4x4x4 slice. The times are simulated.
128 devices in a mesh: row: 16 (over y, x), col: 8 (over z, core).
Axes of the slice: x: 4, y: 4, z: 4, core: 2. Of those that a mesh axis runs over, the one named last changes fastest.
Arguments:
- tokens: bfloat16 [16384, 1280], P(('row', 'col')), may hold values from -6 to 6
- image_sizes: int32 [16, 8], replicated, may hold values from 1 to 48, 256 in all within a row
- slot_of: int32 [128], replicated, may hold values from 0 to 127, as said below
- ln_gain: float32 [1, 2, 1280], replicated, may hold values from 0.25 to 1.75
- ln_bias: float32 [1, 2, 1280], replicated, may hold values from -3 to 3
- w_qkv: bfloat16 [1, 1280, 3840], P(None, 'row', 'col')
- w_out: bfloat16 [1, 1280, 1280], P(None, 'col', 'row'), may hold values from -0.15625 to 0.15625
- w_up: bfloat16 [1, 1280, 5120], P(None, 'row', 'col'), may hold values from -0.15625 to 0.15625
- w_down: bfloat16 [1, 5120, 1280], P(None, 'col', 'row'), may hold values from -0.078125 to 0.078125
- merge_gain: float32 [1280], replicated, may hold values from 0.25 to 1.75
- merge_bias: float32 [1280], replicated, may hold values from -3 to 3
- w_merge: bfloat16 [5120, 4096], P('row', 'col'), may hold values from -0.078125 to 0.078125
Outputs:
- merged_out: bfloat16 [6144, 4096], P('row', 'col')
- req_norm: float32 [128], P('row')
- req_max: float32 [128], P('row')
Inputs may be any that keep to these rules, and one draw needn't show every extreme that they name: Each row of image_sizes sums to 256 and holds 48 at least once. A permutation of the slots. Request g * 8 + j goes to the row group slot_of // 8, which holds 8 slots. No row group sends more than one request to any row group.
All inputs are finite; a program needn't handle non-finite values.
Results may differ from a plain program's by a relative error of at most 0.018.
The roundings to bfloat16 on the way count: a program that leaves them out, or rounds other values in their place, can miss the bound.
Values may be sent and summed in bfloat16 or wider, within the bound.
A program may use at most 64 MiB of HBM per device.

v0:
```python
import jax
import jax.numpy as jnp
from jax import lax
from jax.sharding import PartitionSpec as P

D = 1280
HEAD_DIM = 80
OUT = 4096
IMG_ROW = 8


def layer_norm(values, gain, bias):
    center = jnp.mean(values, axis=-1, keepdims=True)
    shifted = values - center
    spread = jnp.mean(shifted * shifted, axis=-1, keepdims=True)
    return shifted * lax.rsqrt(spread + 1e-06) * gain + bias


def segment_ids(sizes_row, count):
    bounds = jnp.cumsum(sizes_row)
    merged_index = jnp.arange(count, dtype=jnp.int32) // 4
    return jnp.sum((merged_index[:, None] >= bounds[None, :]).astype(jnp.int32), axis=1)


def attend(qkv, segments):
    count = qkv.shape[0]
    width = min(512, count)
    query = qkv[:, :, 0]
    keys = qkv[:, :, 1]
    values = qkv[:, :, 2]
    results = []
    for offset in range(0, count, width):
        scores = jnp.einsum(
            "qhd,khd->hqk", query[offset : offset + width], keys, preferred_element_type=jnp.float32
        ) * HEAD_DIM ** (-0.5)
        same = segments[offset : offset + width, None] == segments[None, :]
        scores = jnp.where(same[None], scores, -1e30)
        peak = jnp.max(scores, axis=-1, keepdims=True)
        expo = jnp.exp(scores - peak)
        weights = (expo / jnp.sum(expo, axis=-1, keepdims=True)).astype(jnp.bfloat16)
        context = jnp.einsum("hqk,khd->qhd", weights, values, preferred_element_type=jnp.float32)
        results.append(context.astype(jnp.bfloat16).reshape(width, -1))
    return jnp.concatenate(results, axis=0)


def local(
    tokens,
    image_sizes,
    slot_of,
    ln_gain,
    ln_bias,
    w_qkv,
    w_out,
    w_up,
    w_down,
    merge_gain,
    merge_bias,
    w_merge,
):
    n_col = lax.axis_size("col")
    row_index = lax.axis_index("row")
    tok_dev = tokens.shape[0]
    tok_row = tok_dev * n_col
    merged_row = tok_row // 4
    most = merged_row * 3 // 16
    sizes_here = lax.dynamic_index_in_dim(image_sizes, row_index, 0, keepdims=False)
    segments = segment_ids(sizes_here, tok_row)
    stream = tokens
    normed = layer_norm(stream.astype(jnp.float32), ln_gain[0, 0], ln_bias[0, 0]).astype(
        jnp.bfloat16
    )
    normed_all = lax.all_gather(normed, "col", axis=0, tiled=True)
    left_part = normed_all
    qkv = jnp.dot(
        left_part,
        lax.all_gather(w_qkv[0], "row", axis=0, tiled=True),
        preferred_element_type=jnp.float32,
    )
    qkv = qkv.astype(jnp.bfloat16).reshape(tok_row, -1, 3, HEAD_DIM)
    context = attend(qkv, segments)
    attn_terms = jnp.dot(
        context,
        lax.all_gather(w_out[0], "row", axis=1, tiled=True),
        preferred_element_type=jnp.float32,
    )
    attn_out = lax.psum_scatter(
        attn_terms.astype(jnp.bfloat16), "col", scatter_dimension=0, tiled=True
    ).astype(jnp.float32)
    stream = (stream.astype(jnp.float32) + attn_out).astype(jnp.bfloat16)
    normed = layer_norm(stream.astype(jnp.float32), ln_gain[0, 1], ln_bias[0, 1]).astype(
        jnp.bfloat16
    )
    normed_mlp = lax.all_gather(normed, "col", axis=0, tiled=True)
    left_part = normed_mlp
    up_value = jnp.dot(
        left_part,
        lax.all_gather(w_up[0], "row", axis=0, tiled=True),
        preferred_element_type=jnp.float32,
    )
    hidden = jax.nn.gelu(up_value, approximate=False).astype(jnp.bfloat16)
    mlp_terms = jnp.dot(
        hidden,
        lax.all_gather(w_down[0], "row", axis=1, tiled=True),
        preferred_element_type=jnp.float32,
    )
    mlp_out = lax.psum_scatter(
        mlp_terms.astype(jnp.bfloat16), "col", scatter_dimension=0, tiled=True
    ).astype(jnp.float32)
    stream = (stream.astype(jnp.float32) + mlp_out).astype(jnp.bfloat16)
    merged = layer_norm(stream.astype(jnp.float32), merge_gain, merge_bias).astype(jnp.bfloat16)
    merged = merged.reshape(tok_dev // 4, 4 * D)
    merged_all = lax.all_gather(merged, "col", axis=0, tiled=True)
    out_dev = w_merge.shape[1]
    left_part = merged_all
    projected = jnp.dot(
        left_part,
        lax.all_gather(w_merge, "row", axis=0, tiled=True),
        preferred_element_type=jnp.float32,
    ).astype(jnp.bfloat16)
    reqs = slot_of.shape[0]
    numbers = jnp.arange(reqs, dtype=jnp.int32)
    req_at_slot = jnp.sum(
        jnp.where(slot_of[None, :] == numbers[:, None], numbers[None, :], 0), axis=1
    )
    starts = jnp.cumsum(image_sizes, axis=1) - image_sizes
    starts_flat = starts.reshape(-1)
    sizes_flat = image_sizes.reshape(-1)
    inner = jnp.arange(most, dtype=jnp.int32)
    request = lax.dynamic_slice_in_dim(req_at_slot, row_index * IMG_ROW, IMG_ROW)
    group = request // IMG_ROW
    source = ((group * merged_row + starts_flat[request])[:, None] + inner[None, :]).reshape(-1)
    valid = (inner[None, :] < sizes_flat[request][:, None]).reshape(-1)
    rows_init = jnp.zeros((IMG_ROW * most, out_dev), jnp.bfloat16)
    piece = lax.all_gather(projected, "row", axis=0, tiled=True)
    inside = valid & (source >= 0) & (source < piece.shape[0])
    taken = jnp.take(piece, jnp.clip(source, 0, piece.shape[0] - 1), axis=0)
    placed = jnp.where(inside[:, None], taken, rows_init)
    blocks = placed.astype(jnp.float32).reshape(IMG_ROW, most, out_dev)
    squares = jnp.sum(blocks * blocks, axis=(1, 2))
    peaks = jnp.max(jnp.abs(blocks), axis=(1, 2))
    squares = lax.psum(squares, "col")
    peaks = lax.pmax(peaks, "col")
    slot_size = sizes_flat[request].astype(jnp.float32)
    req_norm = jnp.sqrt(squares / (slot_size * OUT) + 1e-06)
    merged_out = (
        (blocks / req_norm[:, None, None]).astype(jnp.bfloat16).reshape(IMG_ROW * most, out_dev)
    )
    return (merged_out, req_norm, peaks)


def solution(mesh):
    in_specs = (
        P(("row", "col"), None),
        P(),
        P(),
        P(),
        P(),
        P(None, "row", "col"),
        P(None, "col", "row"),
        P(None, "row", "col"),
        P(None, "col", "row"),
        P(),
        P(),
        P("row", "col"),
    )
    out_specs = (P("row", "col"), P("row"), P("row"))
    return jax.shard_map(local, mesh=mesh, in_specs=in_specs, out_specs=out_specs, check_vma=False)
```

profile of v0, /device:TPU:1, one launch (start us, length us, event | category | flops | bytes accessed | tf_op | source)
XLA Modules:
  0.0 487.1 jit_solution(6885048592995645499)
XLA Ops:
  9.9 1.2 fusion.45
  11.1 2.0 fusion.48
  15.1 22.5 %all-gather.1 = bf16[1,160,1280]{1,0,2:T(2,128)(2,1)S(1)} all-gather(bf16[1,160,80]{1,0,2:T(2,128)(2,1)S(1)} %copy.48), channel_id=3, replica_groups=mesh['row'=16,'col'=8] {'row'}, dimensions={2}, use_global_device_ids=true | all-gather | bytes 435200 | tf_op jit(solution)/shard_map/all_gather | solution.py:83
  37.6 1.8 copy.49
  40.2 14.8 %all-gather.23.cloned.1.call-done = bf16[1,1280,480]{2,1,0:T(8,128)(2,1)} async-done(((bf16[1,80,480]{2,1,0:T(8,128)(2,1)}), bf16[1,1280,480]{2,1,0:T(8,128)(2,1)}) %all-gather.23.cloned.1.call-update) | async-done | bytes 1228816 | tf_op jit(solution)/shard_map/all_gather | solution.py:76
  55.0 30.0 %all-gather.13.cloned.1.call-done = bf16[1024,1280]{1,0:T(8,128)(2,1)} async-done(((bf16[128,1280]{1,0:T(8,128)(2,1)}), bf16[1024,1280]{1,0:T(8,128)(2,1)}) %all-gather.13.cloned.1.call-update) | async-done | bytes 2621456 | tf_op jit(solution)/shard_map/all_gather | solution.py:72
  85.1 3.6 convolution_convert_fusion.2
  88.6 3.7 fusion.112
  92.3 3.6 fusion.111
  95.9 3.2 fusion.31
  100.2 2.4 convolution_convert_fusion.1
  103.9 31.0 %reduce-scatter.3.cloned.1.call-done = bf16[128,1280]{1,0:T(8,128)(2,1)} async-done(((bf16[1024,1280]{1,0:T(8,128)(2,1)}), bf16[128,1280]{1,0:T(8,128)(2,1)}) %reduce-scatter.3.cloned.1.call-update) | async-done | bytes 327696 | tf_op jit(solution)/shard_map/reduce_scatter | solution.py:86
  137.5 43.5 %all-gather.25.cloned.1.call-done = bf16[1,1280,640]{2,1,0:T(8,128)(2,1)} async-done(((bf16[1,80,640]{2,1,0:T(8,128)(2,1)}), bf16[1,1280,640]{2,1,0:T(8,128)(2,1)}) %all-gather.25.cloned.1.call-update) | async-done | bytes 1638416 | tf_op jit(solution)/shard_map/all_gather | solution.py:97
  181.0 45.1 %all-gather.27.cloned.1.call-done = bf16[1,640,1280]{1,2,0:T(8,128)(2,1)} async-done(((bf16[1,640,80]{1,2,0:T(8,128)(2,1)}), bf16[1,640,1280]{1,2,0:T(8,128)(2,1)}) %all-gather.27.cloned.1.call-update) | async-done | bytes 1638416 | tf_op jit(solution)/shard_map/all_gather | solution.py:103
  226.1 29.3 %all-gather.15.cloned.1.call-done = bf16[1024,1280]{1,0:T(8,128)(2,1)} async-done(((bf16[128,1280]{1,0:T(8,128)(2,1)}), bf16[1024,1280]{1,0:T(8,128)(2,1)}) %all-gather.15.cloned.1.call-update) | async-done | bytes 2621456 | tf_op jit(solution)/shard_map/all_gather | solution.py:93
  255.3 13.0 %convolution_convert_fusion = bf16[1024,1280]{1,0:T(8,128)(2,1)} fusion(bf16[1,640,1280]{1,2,0:T(8,128)(2,1)} %all-gather.27.cloned.1.call-done, bf16[1024,1280]{1,0:T(8,128)(2,1)} %all-gather.15.cloned.1.call-done, bf16[1,1280,640]{2,1,0:T(8,128)(2,1)} %all-gather.25.cloned.1.call-done), kind=kOutput, calls=%fused_computation.12 | convolution fusion | flops 3399352320 | bytes 8519680 | tf_op jit(solution)/shard_map/dot_general | solution.py:101
  269.2 31.4 %reduce-scatter.5.cloned.1.call-done = bf16[128,1280]{1,0:T(8,128)(2,1)} async-done(((bf16[1024,1280]{1,0:T(8,128)(2,1)}), bf16[128,1280]{1,0:T(8,128)(2,1)}) %reduce-scatter.5.cloned.1.call-update) | async-done | bytes 327696 | tf_op jit(solution)/shard_map/reduce_scatter | solution.py:106
  305.1 55.3 %all-gather.19.cloned.1.call-done = bf16[5120,512]{1,0:T(8,128)(2,1)} async-done(((bf16[320,512]{1,0:T(8,128)(2,1)}), bf16[5120,512]{1,0:T(8,128)(2,1)}) %all-gather.19.cloned.1.call-update) | async-done | bytes 5242896 | tf_op jit(solution)/shard_map/all_gather | solution.py:117
  360.4 28.6 %all-gather.17.cloned.1.call-done = bf16[256,5120]{1,0:T(8,128)(2,1)} async-done(((bf16[32,5120]{1,0:T(8,128)(2,1)}), bf16[256,5120]{1,0:T(8,128)(2,1)}) %all-gather.17.cloned.1.call-update) | async-done | bytes 2621456 | tf_op jit(solution)/shard_map/all_gather | solution.py:112
  389.0 5.5 %convolution_convert_fusion.3 = bf16[256,512]{1,0:T(8,128)(2,1)} fusion(bf16[256,5120]{1,0:T(8,128)(2,1)} %all-gather.17.cloned.1.call-done, bf16[5120,512]{1,0:T(8,128)(2,1)} %all-gather.19.cloned.1.call-done), kind=kOutput, calls=%fused_computation.47 | convolution fusion | flops 1342308352 | bytes 8126464 | tf_op jit(solution)/shard_map/dot_general | solution.py:115
  397.0 48.9 %all-gather.21.cloned.1.call-done = bf16[4096,512]{1,0:T(8,128)(2,1)} async-done(((bf16[256,512]{1,0:T(8,128)(2,1)}), bf16[4096,512]{1,0:T(8,128)(2,1)}) %all-gather.21.cloned.1.call-update) | async-done | bytes 4194320 | tf_op jit(solution)/shard_map/all_gather | solution.py:134
  445.8 4.8 gather_fusion.2
  451.2 12.7 %psum.7 = f32[8]{0:T(128)S(1)} all-reduce(f32[8]{0:T(128)S(1)} %reduce_sum.118), channel_id=1, replica_groups=mesh['row'=16,'col'=8] {'col'}, use_global_device_ids=true, to_apply=%region_18.19 | all-reduce | flops 8 | bytes 64 | tf_op jit(solution)/shard_map/psum | solution.py:141
  464.3 15.0 %pmax.7 = f32[8]{0:T(128)} all-reduce(f32[8]{0:T(128)S(1)} %reduce_max.38), channel_id=1, replica_groups=mesh['row'=16,'col'=8] {'col'}, use_global_device_ids=true, to_apply=%region_21.22 | all-reduce | flops 8 | bytes 64 | tf_op jit(solution)/shard_map/pmax | solution.py:142
  (86 shorter events, 20.0 us)
Async XLA Ops:
  7.2 47.9 %all-gather.23.cloned.1.call-start = ((), (), s32[]{:S(2)}) async-start(), calls=%async_computation.9 | async-start | bytes 1392640 | tf_op jit(solution)/shard_map/all_gather | solution.py:76
  7.9 77.2 %all-gather.13.cloned.1.call-start = ((), (), s32[]{:S(2)}) async-start(), calls=%async_computation.2 | async-start | bytes 2949120 | tf_op jit(solution)/shard_map/all_gather | solution.py:72
  13.1 121.8 %reduce-scatter.3.cloned.1.call-start = ((), (), s32[]{:S(2)}) async-start(), calls=%async_computation.3 | async-start | bytes 2949120 | tf_op jit(solution)/shard_map/reduce_scatter | solution.py:86
  95.9 3.4 copy-start.6
  100.2 34.7 %copy-start = (bf16[128,1280]{1,0:T(8,128)(2,1)S(1)}, bf16[128,1280]{1,0:T(8,128)(2,1)}, u32[]{:S(2)}) copy-start(bf16[128,1280]{1,0:T(8,128)(2,1)} %param.12) | copy-start | bytes 983044
  102.7 78.3 %all-gather.25.cloned.1.call-start = ((), (), s32[]{:S(2)}) async-start(), calls=%async_computation.10 | async-start | bytes 1740800 | tf_op jit(solution)/shard_map/all_gather | solution.py:97
  103.3 122.8 %all-gather.27.cloned.1.call-start = ((), (), s32[]{:S(2)}) async-start(), calls=%async_computation.11 | async-start | bytes 1740800 | tf_op jit(solution)/shard_map/all_gather | solution.py:103
  103.8 151.5 %all-gather.15.cloned.1.call-start = ((), (), s32[]{:S(2)}) async-start(), calls=%async_computation.4 | async-start | bytes 2949120 | tf_op jit(solution)/shard_map/all_gather | solution.py:93
  137.3 163.3 %reduce-scatter.5.cloned.1.call-start = ((), (), s32[]{:S(2)}) async-start(), calls=%async_computation.5 | async-start | bytes 2949120 | tf_op jit(solution)/shard_map/reduce_scatter | solution.py:106
  268.3 34.6 %copy-start.2 = (f32[1280]{0:T(1024)S(1)}, f32[1280]{0:T(1024)}, u32[]{:S(2)}) copy-start(f32[1280]{0:T(1024)} %param.22) | copy-start | bytes 15364
  268.3 34.6 %copy-start.3 = (f32[1280]{0:T(1024)S(1)}, f32[1280]{0:T(1024)}, u32[]{:S(2)}) copy-start(f32[1280]{0:T(1024)} %param.21) | copy-start | bytes 15364
  268.4 92.0 %all-gather.19.cloned.1.call-start = ((), (), s32[]{:S(2)}) async-start(), calls=%async_computation.7 | async-start | bytes 5570560 | tf_op jit(solution)/shard_map/all_gather | solution.py:117
  269.1 119.9 %all-gather.17.cloned.1.call-start = ((), (), s32[]{:S(2)}) async-start(), calls=%async_computation.6 | async-start | bytes 2949120 | tf_op jit(solution)/shard_map/all_gather | solution.py:112
  305.1 89.5 %copy-start.1 = (s32[16,8]{0,1:T(8,128)S(1)}, s32[16,8]{0,1:T(8,128)}, u32[]{:S(2)}) copy-start(s32[16,8]{0,1:T(8,128)} %param.13) | copy-start | bytes 1540
  305.1 89.7 %copy-start.5 = (s32[128]{0:T(128)S(1)}, s32[128]{0:T(128)}, u32[]{:S(2)}) copy-start(s32[128]{0:T(128)} %param.14) | copy-start | bytes 1540
  305.1 140.7 %all-gather.21.cloned.1.call-start = ((), (), s32[]{:S(2)}) async-start(), calls=%async_computation.8 | async-start | bytes 4456448 | tf_op jit(solution)/shard_map/all_gather | solution.py:134
  464.0 16.3 %copy-start.4 = (f32[8]{0:T(128)}, f32[8]{0:T(128)S(1)}, u32[]{:S(2)}) copy-start(f32[8]{0:T(128)S(1)} %add_sqrt_fusion) | copy-start | bytes 100
Sparse Core Ops, SparseCore 0:
  10.1 44.8 all-gather.22
  57.3 27.7 all-gather.12
  102.8 32.0 reduce-scatter.2
  136.9 44.0 all-gather.24
  183.0 43.0 all-gather.26
  228.2 27.1 all-gather.14
  268.5 32.0 reduce-scatter.4
  302.7 57.6 all-gather.18
  362.7 26.2 all-gather.16
  394.7 51.1 all-gather.20
where the time goes:
time: 488 us; the launch traced here: 487 us
  waiting for transfers between devices  360 us (74%)
  blocking collectives  50.3 us (10%)
  matrix products  35.8 us (7%)
  between operations  14.4 us (3%)
  other arithmetic  13.2 us (3%)
  local copies, waits for them, and re-layouts  12.6 us (3%)
    all_gather x1, waiting for transfers between devices, local(): lax.all_gather(w_merge, 'row', axis=0, tiled=True)  55.3 us
    all_gather x1, waiting for transfers between devices, local(): piece = lax.all_gather(projected, 'row', axis=0, tiled=True)  48.9 us
    all_gather x1, waiting for transfers between devices, local(): lax.all_gather(w_down[0], 'row', axis=1, tiled=True)  45.1 us
    all_gather x1, waiting for transfers between devices, local(): lax.all_gather(w_up[0], 'row', axis=0, tiled=True)  43.5 us
    reduce_scatter x1, waiting for transfers between devices, local(): lax.psum_scatter(mlp_terms.astype(jnp.bfloat16), 'col', scatter_dimension...  31.4 us
    reduce_scatter x1, waiting for transfers between devices, local(): lax.psum_scatter(attn_terms.astype(jnp.bfloat16), 'col', scatter_dimensio...  31 us
    all_gather x1, waiting for transfers between devices, local(): normed_all = lax.all_gather(normed, 'col', axis=0, tiled=True)  30 us
    all_gather x1, waiting for transfers between devices, local(): normed_mlp = lax.all_gather(normed, 'col', axis=0, tiled=True)  29.3 us
  transfers between devices with their start and end apart: 10, of which 10 were waited for; matrix products, arithmetic and copies ran while one was open for 4% of the time, Pallas kernels for 0%

commit v1 on v0

--- a/solution.py
+++ b/solution.py
@@ -7,6 +7,22 @@
 HEAD_DIM = 80
 OUT = 4096
 IMG_ROW = 8
+
+
+def ring_gather(x, axis, dim):
+    ways, here, lap = (lax.axis_size(axis), lax.axis_index(axis), x.shape[dim])
+    shape = [n * ways if d == dim else n for d, n in enumerate(x.shape)]
+    full = lax.dynamic_update_slice_in_dim(jnp.zeros(shape, x.dtype), x, here * lap, axis=dim)
+    going_up = going_down = x
+    for far in range(1, ways // 2 + 1):
+        going_up = lax.ppermute(going_up, axis, [(d, (d + 1) % ways) for d in range(ways)])
+        full = lax.dynamic_update_slice_in_dim(full, going_up, (here - far) % ways * lap, axis=dim)
+        if 2 * far < ways:
+            going_down = lax.ppermute(going_down, axis, [(d, (d - 1) % ways) for d in range(ways)])
+            full = lax.dynamic_update_slice_in_dim(
+                full, going_down, (here + far) % ways * lap, axis=dim
+            )
+    return full
 
 
 def layer_norm(values, gain, bias):
@@ -69,7 +85,7 @@
     normed = layer_norm(stream.astype(jnp.float32), ln_gain[0, 0], ln_bias[0, 0]).astype(
         jnp.bfloat16
     )
-    normed_all = lax.all_gather(normed, "col", axis=0, tiled=True)
+    normed_all = ring_gather(normed, "col", 0)
     left_part = normed_all
     qkv = jnp.dot(
         left_part,

time: 488 us -> 470 us (0.963)
  waiting for transfers between devices: 360 us -> 324 us
  starting transfers between devices: 0.58 us -> 16.2 us
  local copies, waits for them, and re-layouts: 12.6 us -> 18.1 us
    all_gather x1 -> x0, waiting for transfers between devices: 30 us -> none  [local(): normed_all = lax.all_gather(normed, 'col', axis=0, tiled=True)]
    ppermute x0 -> x7, starting transfers between devices: none -> 15.7 us  [the longest x4 15 us: ring_gather(): lax.ppermute(going_up, axis, [(d, (d + 1) % ways) for d in range(ways)])]
    all_gather x1, waiting for transfers between devices: 14.8 us -> 0.01 us  [local(): lax.all_gather(w_qkv[0], 'row', axis=0, tiled=True)]
    ppermute x0 -> x7, waiting for transfers between devices: none -> 6.87 us  [the longest x4 6.46 us: ring_gather(): lax.ppermute(going_up, axis, [(d, (d + 1) % ways) for d in range(ways)])]
    dynamic_update_slice x0 -> x7, local copies, waits for them, and re-layouts: none -> 5.24 us  [the longest x4 2.96 us: ring_gather(): lax.dynamic_update_slice_in_dim(full, going_up, (here - far) % ways * lap...]
  transfers between devices with their start and end apart: 10 -> 16, of which waited for: 10 -> 12; matrix products, arithmetic and copies ran while one was open for 4% -> 4% of each run, Pallas kernels for 0% -> 0%
where the time goes in v1:
time: 470 us
  waiting for transfers between devices  324 us (69%)
  blocking collectives  49.1 us (10%)
  matrix products  35.8 us (8%)
  local copies, waits for them, and re-layouts  18.1 us (4%)
  starting transfers between devices  16.2 us (3%)
  between operations  14.2 us (3%)
  other arithmetic  12.3 us (3%)
    all_gather x1, waiting for transfers between devices, local(): lax.all_gather(w_merge, 'row', axis=0, tiled=True)  55.3 us
    all_gather x1, waiting for transfers between devices, local(): piece = lax.all_gather(projected, 'row', axis=0, tiled=True)  48.9 us
    all_gather x1, waiting for transfers between devices, local(): lax.all_gather(w_down[0], 'row', axis=1, tiled=True)  45.1 us
    all_gather x1, waiting for transfers between devices, local(): lax.all_gather(w_up[0], 'row', axis=0, tiled=True)  43.6 us
    reduce_scatter x1, waiting for transfers between devices, local(): lax.psum_scatter(attn_terms.astype(jnp.bfloat16), 'col', scatter_dimensio...  32.9 us
    reduce_scatter x1, waiting for transfers between devices, local(): lax.psum_scatter(mlp_terms.astype(jnp.bfloat16), 'col', scatter_dimension...  31.4 us
    all_gather x1, waiting for transfers between devices, local(): normed_mlp = lax.all_gather(normed, 'col', axis=0, tiled=True)  29.3 us
    all_gather x1, waiting for transfers between devices, local(): merged_all = lax.all_gather(merged, 'col', axis=0, tiled=True)  28.6 us
  transfers between devices with their start and end apart: 16, of which 12 were waited for; matrix products, arithmetic and copies ran while one was open for 4% of the time, Pallas kernels for 0%

profile of v1, /device:TPU:1, one launch (start us, length us, event | category | flops | bytes accessed | tf_op | source)
XLA Modules:
  0.0 469.5 jit_solution(10143123524472847171)
XLA Ops:
  13.1 3.0 collective-permute-start
  16.9 21.3 %all-gather.1 = bf16[1,160,1280]{1,0,2:T(2,128)(2,1)S(1)} all-gather(bf16[1,160,80]{1,0,2:T(2,128)(2,1)S(1)} %copy.48), channel_id=3, replica_groups=mesh['row'=16,'col'=8] {'row'}, dimensions={2}, use_global_device_ids=true | all-gather | bytes 435200 | tf_op jit(solution)/shard_map/all_gather | solution.py:99
  40.9 7.0 %collective-permute-start.2 = (bf16[128,1280]{1,0:T(8,128)(2,1)S(1)}, bf16[128,1280]{1,0:T(8,128)(2,1)S(1)}, u32[]{:S(2)}, u32[]{:S(2)}) collective-permute-start(bf16[128,1280]{1,0:T(8,128)(2,1)S(1)} %collective-permute-done), channel_id=1, source_target_pairs={{0,1},{1,2},{2,3},{3,4},{4,5},{5,6},{6,7},{7,0},{8,9},{9,10},{10,1... | collective-permute-start | bytes 983048 | tf_op jit(solution)/shard_map/ppermute | solution.py:18
  49.4 2.5 collective-permute-done.2
  51.9 2.5 collective-permute-start.4
  58.4 2.5 collective-permute-start.6
  62.4 2.5 collective-permute-done.6
  65.6 3.6 convolution_convert_fusion.2
  69.2 3.7 fusion.113
  72.9 3.6 fusion.112
  76.5 3.2 fusion.31
  84.6 32.9 %reduce-scatter.3.cloned.1.call-done = bf16[128,1280]{1,0:T(8,128)(2,1)} async-done(((bf16[1024,1280]{1,0:T(8,128)(2,1)}), bf16[128,1280]{1,0:T(8,128)(2,1)}) %reduce-scatter.3.cloned.1.call-update) | async-done | bytes 327696 | tf_op jit(solution)/shard_map/reduce_scatter | solution.py:102
  120.2 43.6 %all-gather.22.cloned.1.call-done = bf16[1,1280,640]{2,1,0:T(8,128)(2,1)} async-done(((bf16[1,80,640]{2,1,0:T(8,128)(2,1)}), bf16[1,1280,640]{2,1,0:T(8,128)(2,1)}) %all-gather.22.cloned.1.call-update) | async-done | bytes 1638416 | tf_op jit(solution)/shard_map/all_gather | solution.py:113
  163.8 45.1 %all-gather.24.cloned.1.call-done = bf16[1,640,1280]{1,2,0:T(8,128)(2,1)} async-done(((bf16[1,640,80]{1,2,0:T(8,128)(2,1)}), bf16[1,640,1280]{1,2,0:T(8,128)(2,1)}) %all-gather.24.cloned.1.call-update) | async-done | bytes 1638416 | tf_op jit(solution)/shard_map/all_gather | solution.py:119
  208.8 29.3 %all-gather.12.cloned.1.call-done = bf16[1024,1280]{1,0:T(8,128)(2,1)} async-done(((bf16[128,1280]{1,0:T(8,128)(2,1)}), bf16[1024,1280]{1,0:T(8,128)(2,1)}) %all-gather.12.cloned.1.call-update) | async-done | bytes 2621456 | tf_op jit(solution)/shard_map/all_gather | solution.py:109
  238.1 13.0 %convolution_convert_fusion = bf16[1024,1280]{1,0:T(8,128)(2,1)} fusion(bf16[1,640,1280]{1,2,0:T(8,128)(2,1)} %all-gather.24.cloned.1.call-done, bf16[1024,1280]{1,0:T(8,128)(2,1)} %all-gather.12.cloned.1.call-done, bf16[1,1280,640]{2,1,0:T(8,128)(2,1)} %all-gather.22.cloned.1.call-done), kind=kOutput, calls=%fused_computation.12 | convolution fusion | flops 3399352320 | bytes 8519680 | tf_op jit(solution)/shard_map/dot_general | solution.py:117
  251.9 31.4 %reduce-scatter.5.cloned.1.call-done = bf16[128,1280]{1,0:T(8,128)(2,1)} async-done(((bf16[1024,1280]{1,0:T(8,128)(2,1)}), bf16[128,1280]{1,0:T(8,128)(2,1)}) %reduce-scatter.5.cloned.1.call-update) | async-done | bytes 327696 | tf_op jit(solution)/shard_map/reduce_scatter | solution.py:122
  287.9 55.3 %all-gather.16.cloned.1.call-done = bf16[5120,512]{1,0:T(8,128)(2,1)} async-done(((bf16[320,512]{1,0:T(8,128)(2,1)}), bf16[5120,512]{1,0:T(8,128)(2,1)}) %all-gather.16.cloned.1.call-update) | async-done | bytes 5242896 | tf_op jit(solution)/shard_map/all_gather | solution.py:133
  343.2 28.6 %all-gather.14.cloned.1.call-done = bf16[256,5120]{1,0:T(8,128)(2,1)} async-done(((bf16[32,5120]{1,0:T(8,128)(2,1)}), bf16[256,5120]{1,0:T(8,128)(2,1)}) %all-gather.14.cloned.1.call-update) | async-done | bytes 2621456 | tf_op jit(solution)/shard_map/all_gather | solution.py:128
  371.8 5.5 %convolution_convert_fusion.3 = bf16[256,512]{1,0:T(8,128)(2,1)} fusion(bf16[256,5120]{1,0:T(8,128)(2,1)} %all-gather.14.cloned.1.call-done, bf16[5120,512]{1,0:T(8,128)(2,1)} %all-gather.16.cloned.1.call-done), kind=kOutput, calls=%fused_computation.47 | convolution fusion | flops 1342308352 | bytes 8126464 | tf_op jit(solution)/shard_map/dot_general | solution.py:131
  379.7 48.9 %all-gather.18.cloned.1.call-done = bf16[4096,512]{1,0:T(8,128)(2,1)} async-done(((bf16[256,512]{1,0:T(8,128)(2,1)}), bf16[4096,512]{1,0:T(8,128)(2,1)}) %all-gather.18.cloned.1.call-update) | async-done | bytes 4194320 | tf_op jit(solution)/shard_map/all_gather | solution.py:150
  428.6 4.8 %gather_fusion.2 = bf16[384,512]{1,0:T(8,128)(2,1)S(1)} fusion(bf16[4096,512]{1,0:T(8,128)(2,1)} %all-gather.18.cloned.1.call-done, s32[1024]{0:T(1024)S(1)} %pad_clamp_fusion), kind=kCustom, calls=%fused_computation.2 | custom fusion | bytes 787968 | tf_op jit(solution)/shard_map/jit(_take)/gather | solution.py:152
  434.0 12.7 %psum.7 = f32[8]{0:T(128)S(1)} all-reduce(f32[8]{0:T(128)S(1)} %reduce_sum.118), channel_id=1, replica_groups=mesh['row'=16,'col'=8] {'col'}, use_global_device_ids=true, to_apply=%region_18.19 | all-reduce | flops 8 | bytes 64 | tf_op jit(solution)/shard_map/psum | solution.py:157
  447.1 15.0 %pmax.7 = f32[8]{0:T(128)} all-reduce(f32[8]{0:T(128)S(1)} %reduce_max.38), channel_id=1, replica_groups=mesh['row'=16,'col'=8] {'col'}, use_global_device_ids=true, to_apply=%region_21.22 | all-reduce | flops 8 | bytes 64 | tf_op jit(solution)/shard_map/pmax | solution.py:158
  (107 shorter events, 33.9 us)
Async XLA Ops:
  7.2 5.0 %copy-start = (bf16[128,1280]{1,0:T(8,128)(2,1)S(1)}, bf16[128,1280]{1,0:T(8,128)(2,1)}, u32[]{:S(2)}) copy-start(bf16[128,1280]{1,0:T(8,128)(2,1)} %param.12) | copy-start | bytes 983044
  7.2 9.1 %copy-start.1 = (s32[16,8]{0,1:T(8,128)S(1)}, s32[16,8]{0,1:T(8,128)}, u32[]{:S(2)}) copy-start(s32[16,8]{0,1:T(8,128)} %param.13) | copy-start | bytes 1540
  7.2 9.5 %copy-start.2 = (bf16[1,160,80]{2,1,0:T(8,128)(2,1)S(1)}, bf16[1,160,80]{2,1,0:T(8,128)(2,1)}, u32[]{:S(2)}) copy-start(bf16[1,160,80]{2,1,0:T(8,128)(2,1)} %param.18) | copy-start | bytes 76804
  7.2 58.4 %all-gather.20.cloned.1.call-start = ((), (), s32[]{:S(2)}) async-start(), calls=%async_computation.8 | async-start | bytes 1392640 | tf_op jit(solution)/shard_map/all_gather | solution.py:92
  13.1 27.7 %collective-permute-start = (bf16[128,1280]{1,0:T(8,128)(2,1)S(1)}, bf16[128,1280]{1,0:T(8,128)(2,1)S(1)}, u32[]{:S(2)}, u32[]{:S(2)}) collective-permute-start(bf16[128,1280]{1,0:T(8,128)(2,1)S(1)} %get-tuple-element.13), channel_id=1, source_target_pairs={{0,1},{1,2},{2,3},{3,4},{4,5},{5,6},{6,7},{7,0},{8,9},{9,10},{10,1... | collective-permute-start | bytes 983048 | tf_op jit(solution)/shard_map/ppermute | solution.py:18
  16.2 31.7 %collective-permute-start.1 = (bf16[128,1280]{1,0:T(8,128)(2,1)S(1)}, bf16[128,1280]{1,0:T(8,128)(2,1)S(1)}, u32[]{:S(2)}, u32[]{:S(2)}) collective-permute-start(bf16[128,1280]{1,0:T(8,128)(2,1)S(1)} %get-tuple-element.13), channel_id=1, source_target_pairs={{0,7},{1,0},{2,1},{3,2},{4,3},{5,4},{6,5},{7,6},{8,15},{9,8},{10,9... | collective-permute-start | bytes 983048 | tf_op jit(solution)/shard_map/ppermute | solution.py:21
  16.2 101.3 %reduce-scatter.3.cloned.1.call-start = ((), (), s32[]{:S(2)}) async-start(), calls=%async_computation.2 | async-start | bytes 2949120 | tf_op jit(solution)/shard_map/reduce_scatter | solution.py:102
  40.9 11.0 %collective-permute-start.2 = (bf16[128,1280]{1,0:T(8,128)(2,1)S(1)}, bf16[128,1280]{1,0:T(8,128)(2,1)S(1)}, u32[]{:S(2)}, u32[]{:S(2)}) collective-permute-start(bf16[128,1280]{1,0:T(8,128)(2,1)S(1)} %collective-permute-done), channel_id=1, source_target_pairs={{0,1},{1,2},{2,3},{3,4},{4,5},{5,6},{6,7},{7,0},{8,9},{9,10},{10,1... | collective-permute-start | bytes 983048 | tf_op jit(solution)/shard_map/ppermute | solution.py:18
  47.9 6.9 %collective-permute-start.3 = (bf16[128,1280]{1,0:T(8,128)(2,1)S(1)}, bf16[128,1280]{1,0:T(8,128)(2,1)S(1)}, u32[]{:S(2)}, u32[]{:S(2)}) collective-permute-start(bf16[128,1280]{1,0:T(8,128)(2,1)S(1)} %collective-permute-done.1), channel_id=1, source_target_pairs={{0,7},{1,0},{2,1},{3,2},{4,3},{5,4},{6,5},{7,6},{8,15},{9,8},{10,9... | collective-permute-start | bytes 983048 | tf_op jit(solution)/shard_map/ppermute | solution.py:21
  51.9 6.5 %collective-permute-start.4 = (bf16[128,1280]{1,0:T(8,128)(2,1)S(1)}, bf16[128,1280]{1,0:T(8,128)(2,1)S(1)}, u32[]{:S(2)}, u32[]{:S(2)}) collective-permute-start(bf16[128,1280]{1,0:T(8,128)(2,1)S(1)} %collective-permute-done.2), channel_id=1, source_target_pairs={{0,1},{1,2},{2,3},{3,4},{4,5},{5,6},{6,7},{7,0},{8,9},{9,10},{10,1... | collective-permute-start | bytes 983048 | tf_op jit(solution)/shard_map/ppermute | solution.py:18
  54.8 6.9 %collective-permute-start.5 = (bf16[128,1280]{1,0:T(8,128)(2,1)S(1)}, bf16[128,1280]{1,0:T(8,128)(2,1)S(1)}, u32[]{:S(2)}, u32[]{:S(2)}) collective-permute-start(bf16[128,1280]{1,0:T(8,128)(2,1)S(1)} %collective-permute-done.3), channel_id=1, source_target_pairs={{0,7},{1,0},{2,1},{3,2},{4,3},{5,4},{6,5},{7,6},{8,15},{9,8},{10,9... | collective-permute-start | bytes 983048 | tf_op jit(solution)/shard_map/ppermute | solution.py:21
  58.4 6.5 %collective-permute-start.6 = (bf16[128,1280]{1,0:T(8,128)(2,1)S(1)}, bf16[128,1280]{1,0:T(8,128)(2,1)S(1)}, u32[]{:S(2)}, u32[]{:S(2)}) collective-permute-start(bf16[128,1280]{1,0:T(8,128)(2,1)S(1)} %collective-permute-done.4), channel_id=1, source_target_pairs={{0,1},{1,2},{2,3},{3,4},{4,5},{5,6},{6,7},{7,0},{8,9},{9,10},{10,1... | collective-permute-start | bytes 983048 | tf_op jit(solution)/shard_map/ppermute | solution.py:18
  76.5 3.4 copy-start.7
  83.3 80.5 %all-gather.22.cloned.1.call-start = ((), (), s32[]{:S(2)}) async-start(), calls=%async_computation.9 | async-start | bytes 1740800 | tf_op jit(solution)/shard_map/all_gather | solution.py:113
  84.0 124.8 %all-gather.24.cloned.1.call-start = ((), (), s32[]{:S(2)}) async-start(), calls=%async_computation.10 | async-start | bytes 1740800 | tf_op jit(solution)/shard_map/all_gather | solution.py:119
  84.6 153.5 %all-gather.12.cloned.1.call-start = ((), (), s32[]{:S(2)}) async-start(), calls=%async_computation.3 | async-start | bytes 2949120 | tf_op jit(solution)/shard_map/all_gather | solution.py:109
  119.9 163.4 %reduce-scatter.5.cloned.1.call-start = ((), (), s32[]{:S(2)}) async-start(), calls=%async_computation.4 | async-start | bytes 2949120 | tf_op jit(solution)/shard_map/reduce_scatter | solution.py:122
  251.1 34.5 %copy-start.3 = (f32[1280]{0:T(1024)S(1)}, f32[1280]{0:T(1024)}, u32[]{:S(2)}) copy-start(f32[1280]{0:T(1024)} %param.22) | copy-start | bytes 15364
  251.1 34.5 %copy-start.4 = (f32[1280]{0:T(1024)S(1)}, f32[1280]{0:T(1024)}, u32[]{:S(2)}) copy-start(f32[1280]{0:T(1024)} %param.21) | copy-start | bytes 15364
  251.1 92.0 %all-gather.16.cloned.1.call-start = ((), (), s32[]{:S(2)}) async-start(), calls=%async_computation.6 | async-start | bytes 5570560 | tf_op jit(solution)/shard_map/all_gather | solution.py:133
  251.9 119.9 %all-gather.14.cloned.1.call-start = ((), (), s32[]{:S(2)}) async-start(), calls=%async_computation.5 | async-start | bytes 2949120 | tf_op jit(solution)/shard_map/all_gather | solution.py:128
  287.8 89.8 %copy-start.6 = (s32[128]{0:T(128)S(1)}, s32[128]{0:T(128)}, u32[]{:S(2)}) copy-start(s32[128]{0:T(128)} %param.14) | copy-start | bytes 1540
  287.8 140.8 %all-gather.18.cloned.1.call-start = ((), (), s32[]{:S(2)}) async-start(), calls=%async_computation.7 | async-start | bytes 4456448 | tf_op jit(solution)/shard_map/all_gather | solution.py:150
  446.7 16.3 %copy-start.5 = (f32[8]{0:T(128)}, f32[8]{0:T(128)S(1)}, u32[]{:S(2)}) copy-start(f32[8]{0:T(128)S(1)} %add_sqrt_fusion) | copy-start | bytes 100
Sparse Core Ops, SparseCore 0:
  16.3 43.4 all-gather.19
  83.4 34.0 reduce-scatter.2
  119.6 44.0 all-gather.21
  165.8 43.0 all-gather.23
  211.0 27.1 all-gather.11
  251.3 31.9 reduce-scatter.4
  285.4 57.6 all-gather.15
  345.4 26.2 all-gather.13
  377.4 51.1 all-gather.17
